TPU v7x, 32 devices: a whole 2x2x4 slice. The times are simulated.
32 devices in a mesh: tile: 4 (over y, core), dp: 8 (over z, x).
Axes of the slice: x: 2, y: 2, z: 4, core: 2. Of those that a mesh axis runs over, the one named last changes fastest.
Arguments:
- observed: float32 [8, 2, 8, 32], P('dp', None, 'tile'), may hold values from -6 to 6
- targets: float32 [8, 2, 8, 32], P('dp', None, 'tile'), may hold values from -6 to 6
- pixel_mask: int32 [8, 2, 8, 32], P('dp', None, 'tile'), may hold values 0 or 1
- lengths: int32 [8], P('dp'), may hold values from 1 to 2, as said below
- step_count: int32 [1], replicated, may hold values from 2 to 20
- kernels: float32 [1, 12800, 1024], P(None, 'dp'), may hold values from -0.0546875 to 0.0546875
- kernel_moment: float32 [1, 12800, 1024], P(None, 'dp'), may hold values from -7.6293945e-06 to 7.6293945e-06
- kernel_second: float32 [1, 12800, 1024], P(None, 'dp'), may hold values from 1.9073486e-12 to 7.6293945e-12
- norm_params: float32 [2, 1, 1024], replicated
- norm_moment: float32 [2, 1, 1024], replicated, may hold values from -1.5258789e-05 to 1.5258789e-05
- norm_second: float32 [2, 1, 1024], replicated, may hold values from 7.6293945e-12 to 3.0517578e-11
- end_params: float32 [3, 256], replicated
- end_moment: float32 [3, 256], replicated, may hold values from -7.6293945e-05 to 7.6293945e-05
- end_second: float32 [3, 256], replicated, may hold values from 1.9073486e-10 to 7.6293943e-10
- head_bias: float32 [1], replicated, may hold values from -3 to 3
- head_moment: float32 [1], replicated, may hold values from -0.0546875 to 0.0546875
- head_second: float32 [1], replicated, may hold values from 7.6293945e-05 to 0.00030517578
- hidden_init: float32 [1, 8, 8, 32, 256], P(None, 'dp', 'tile'), may hold values from -0.9 to 0.9
- cells_init: float32 [1, 8, 8, 32, 256], P(None, 'dp', 'tile'), may hold values from -5 to 5
Outputs:
- loss_value: float32 [], replicated
- grad_norm: float32 [], replicated
- kernels_new: float32 [1, 12800, 1024], P(None, 'dp')
- kernel_moment_new: float32 [1, 12800, 1024], P(None, 'dp')
- kernel_second_new: float32 [1, 12800, 1024], P(None, 'dp')
- norm_new: float32 [2, 1, 1024], replicated
- norm_moment_new: float32 [2, 1, 1024], replicated
- norm_second_new: float32 [2, 1, 1024], replicated
- end_new: float32 [3, 256], replicated
- end_moment_new: float32 [3, 256], replicated
- end_second_new: float32 [3, 256], replicated
- head_new: float32 [1], replicated
- head_moment_new: float32 [1], replicated
- head_second_new: float32 [1], replicated
- hidden_final: float32 [1, 8, 8, 32, 256], P(None, 'dp', 'tile')
- cells_final: float32 [1, 8, 8, 32, 256], P(None, 'dp', 'tile')
Inputs may be any that keep to these rules, and one draw needn't show every extreme that they name: `lengths`: some stream has all 2 frames counting and some only one.
All inputs are finite; a program needn't handle non-finite values. No bound on the sum of `pixel_mask` on one device may be relied on, other than what follows from the above.
Results may differ from a plain program's by a relative error of at most 0.0003.
The roundings to bfloat16 on the way count: a program that leaves them out, or rounds other values in their place, can miss the bound.
Values may be sent and summed in bfloat16 or wider, within the bound.
No kernel may reach another device: no remote copies, remote signals or barrier semaphores. Data moves between devices by JAX's collectives and lax.ppermute only.
A program may use at most 192 MiB of HBM per device.

v0:
```python
import jax
import jax.numpy as jnp
from jax import lax
from jax.sharding import PartitionSpec as P

IN_DIM = 512
KERNEL = 5
GROUP_SIZE = 64
clip_limit = 0.005
small_rate = 0.1


def padded_2(cells, sides, width):
    for axis, dim in sides:
        count = lax.axis_size(axis)
        ends = count - 1
        head = lax.slice_in_dim(cells, 0, width, axis=dim)
        tail = lax.slice_in_dim(cells, cells.shape[dim] - width, cells.shape[dim], axis=dim)
        cells = jnp.concatenate(
            [
                lax.ppermute(tail, axis, [(i, (i + 1) % count) for i in range(ends)]),
                cells,
                lax.ppermute(head, axis, [((i + 1) % count, i) for i in range(ends)]),
            ],
            axis=dim,
        )
    return cells


def group_norm(gates, gain, shift):
    full_shape = gates.shape
    grouped = gates.reshape(full_shape[:-1] + (full_shape[-1] // GROUP_SIZE, GROUP_SIZE))
    centred = grouped - jnp.mean(grouped, axis=-1, keepdims=True)
    spread = jnp.mean(centred * centred, axis=-1, keepdims=True)
    return (centred * lax.rsqrt(spread + 1e-05)).reshape(full_shape) * gain + shift


def lstm_cell(gates, cells_prev, gain, shift):
    normed = group_norm(gates, gain, shift)
    quarter = normed.shape[-1] // 4
    input_gate = jax.nn.sigmoid(normed[..., :quarter])
    forget_gate = jax.nn.sigmoid(normed[..., quarter : 2 * quarter])
    candidate = jnp.tanh(normed[..., 2 * quarter : 3 * quarter])
    output_gate = jax.nn.sigmoid(normed[..., 3 * quarter :])
    cells_next = forget_gate * cells_prev + input_gate * candidate
    return (output_gate * jnp.tanh(cells_next), cells_next)


def unfold(padded, rows, columns):
    pieces = []
    for row_off in range(KERNEL):
        for col_off in range(KERNEL):
            pieces.append(padded[:, row_off : row_off + rows, col_off : col_off + columns, :])
    joined = jnp.concatenate(pieces, axis=-1)
    return joined.reshape(-1, joined.shape[-1])


def pad_columns(values):
    margin = KERNEL // 2
    return jnp.pad(values, ((0, 0), (0, 0), (margin, margin), (0, 0)))


def layer_forward(weight_full, gain, shift, inputs_low, hidden_start, cells_start):
    rows, columns = (hidden_start.shape[1], hidden_start.shape[2])
    hidden_low = hidden_start.astype(jnp.bfloat16)
    cells = cells_start
    kept = []
    outputs = []
    outputs_low = []
    hidden = hidden_start
    for frame_no in range(len(inputs_low)):
        joined = jnp.concatenate([inputs_low[frame_no], hidden_low], axis=-1)
        padded = padded_2(joined, (("tile", 1),), KERNEL // 2)
        padded = pad_columns(padded)
        gates = jnp.dot(
            unfold(padded, rows, columns), weight_full, preferred_element_type=jnp.float32
        )
        gates = gates.reshape(hidden_start.shape[:3] + (weight_full.shape[1],))
        kept.append((padded, gates, cells))
        hidden, cells = lstm_cell(gates, cells, gain, shift)
        hidden_low = hidden.astype(jnp.bfloat16)
        outputs.append(hidden)
        outputs_low.append(hidden_low)
    return (outputs, outputs_low, kept, hidden, cells)


def layer_backward(weight_full, gain, shift, kept, grad_above):
    pixel_shape = kept[0][1].shape
    rows, columns, gate_dim = (pixel_shape[1], pixel_shape[2], pixel_shape[3])
    in_dim = weight_full.shape[0] // (KERNEL * KERNEL)
    half = in_dim // 2
    flipped = weight_full.reshape(KERNEL, KERNEL, in_dim, gate_dim)[::-1, ::-1]
    flipped = flipped.transpose(0, 1, 3, 2).reshape(KERNEL * KERNEL * gate_dim, in_dim)
    grad_weight = jnp.zeros(weight_full.shape, jnp.float32)
    grad_gain = jnp.zeros(gain.shape, jnp.float32)
    grad_shift = jnp.zeros(shift.shape, jnp.float32)
    grad_hidden = jnp.zeros(pixel_shape[:3] + (half,), jnp.float32)
    grad_cells = jnp.zeros(pixel_shape[:3] + (half,), jnp.float32)
    grad_inputs = [None] * len(kept)
    for frame_no in reversed(range(len(kept))):
        padded, gates, cells_prev = kept[frame_no]
        unused, pull = jax.vjp(lstm_cell, gates, cells_prev, gain, shift)
        grad_gates, grad_cells, part_gain, part_shift = pull(
            (grad_above[frame_no] + grad_hidden, grad_cells)
        )
        grad_gain = grad_gain + part_gain
        grad_shift = grad_shift + part_shift
        gates_low = grad_gates.astype(jnp.bfloat16)
        grad_weight = grad_weight + lax.dot_general(
            unfold(padded, rows, columns),
            gates_low.reshape(-1, gate_dim),
            (((0,), (0,)), ((), ())),
            preferred_element_type=jnp.float32,
        )
        spread = padded_2(gates_low, (("tile", 1),), KERNEL // 2)
        spread = pad_columns(spread)
        grad_joined = jnp.dot(
            unfold(spread, rows, columns), flipped, preferred_element_type=jnp.float32
        )
        grad_joined = grad_joined.reshape(pixel_shape[:3] + (in_dim,))
        grad_inputs[frame_no] = grad_joined[..., :half]
        grad_hidden = grad_joined[..., half:]
    return (grad_weight, grad_gain, grad_shift, grad_inputs)


def adamw(weight, moment, second, grad, rate, correction):
    moment_new = 0.5 * moment + 0.5 * grad
    second_new = 0.5 * second + 0.5 * grad * grad
    update = moment_new / correction / (jnp.sqrt(second_new / correction) + 1e-08)
    return (weight - rate * (update + 0.01 * weight), moment_new, second_new)


def per_device(
    observed,
    targets,
    pixel_mask,
    lengths,
    step_count,
    kernels,
    kernel_moment,
    kernel_second,
    norm_params,
    norm_moment,
    norm_second,
    end_params,
    end_moment,
    end_second,
    head_bias,
    head_moment,
    head_second,
    hidden_init,
    cells_init,
):
    frame_total = observed.shape[1]
    layers = kernels.shape[0]
    frame_ids = lax.broadcasted_iota(jnp.int32, (1, frame_total), 1)
    counted = (frame_ids < lengths[:, None]).astype(jnp.float32)
    valid = pixel_mask.astype(jnp.float32) * counted[:, :, None, None]
    count = jnp.maximum(lax.psum(jnp.sum(valid), ("tile", "dp")), 1.0)
    inputs_low = [
        (end_params[0] * observed[:, frame_no, :, :, None] + end_params[1]).astype(jnp.bfloat16)
        for frame_no in range(frame_total)
    ]
    outputs = []
    layer_no = 0
    weight_full = lax.all_gather(kernels[layer_no].astype(jnp.bfloat16), "dp", axis=0, tiled=True)
    outputs, outputs_low, kept, hidden, cells = layer_forward(
        weight_full,
        norm_params[0, layer_no],
        norm_params[1, layer_no],
        inputs_low,
        hidden_init[layer_no],
        cells_init[layer_no],
    )
    stored_kept = [kept]
    hidden_list = [hidden]
    cells_list = [cells]
    loss_sum = jnp.zeros((), jnp.float32)
    grad_head_weight = jnp.zeros(end_params.shape[1:], jnp.float32)
    grad_head = jnp.zeros((1,), jnp.float32)
    grad_above = []
    for frame_no in range(frame_total):
        predicted = jnp.sum(outputs[frame_no] * end_params[2], axis=-1) + head_bias[0]
        error = predicted - targets[:, frame_no]
        weighted = valid[:, frame_no] * error
        loss_sum = loss_sum + jnp.sum(weighted * error)
        grad_pred = 2.0 * weighted / count
        grad_head = grad_head + jnp.sum(grad_pred)
        grad_head_weight = grad_head_weight + jnp.sum(
            grad_pred[..., None] * outputs[frame_no], axis=(0, 1, 2)
        )
        grad_above.append(grad_pred[..., None] * end_params[2])
    kernel_grads = [None] * layers
    gain_grads = [None] * layers
    shift_grads = [None] * layers
    for layer_no in reversed(range(layers)):
        weight_full = lax.all_gather(
            kernels[layer_no].astype(jnp.bfloat16), "dp", axis=0, tiled=True
        )
        grad_weight, grad_gain, grad_shift, grad_inputs = layer_backward(
            weight_full,
            norm_params[0, layer_no],
            norm_params[1, layer_no],
            stored_kept[layer_no],
            grad_above,
        )
        kernel_grads[layer_no] = grad_weight
        gain_grads[layer_no] = grad_gain
        shift_grads[layer_no] = grad_shift
        grad_above = grad_inputs
    grad_lift_weight = jnp.zeros(end_params.shape[1:], jnp.float32)
    grad_lift_bias = jnp.zeros(end_params.shape[1:], jnp.float32)
    for frame_no in range(frame_total):
        grad_lift_weight = grad_lift_weight + jnp.sum(
            grad_above[frame_no] * observed[:, frame_no, :, :, None], axis=(0, 1, 2)
        )
        grad_lift_bias = grad_lift_bias + jnp.sum(grad_above[frame_no], axis=(0, 1, 2))
    grad_norms = jnp.stack([jnp.stack(gain_grads), jnp.stack(shift_grads)])
    grad_ends = jnp.stack([grad_lift_weight, grad_lift_bias, grad_head_weight])
    grad_kernels = jnp.stack(kernel_grads)
    shard = lax.psum_scatter(grad_kernels, "dp", scatter_dimension=1, tiled=True)
    shard = lax.psum(shard, "tile")
    local_square = jnp.sum(shard * shard)
    grad_norms, grad_ends, grad_head, loss_sum = lax.psum(
        (grad_norms, grad_ends, grad_head, loss_sum), ("tile", "dp")
    )
    kernel_square = lax.psum(local_square, "dp")
    squares = (
        kernel_square
        + jnp.sum(grad_norms * grad_norms)
        + jnp.sum(grad_ends * grad_ends)
        + jnp.sum(grad_head * grad_head)
    )
    grad_norm = jnp.sqrt(squares)
    factor = clip_limit / jnp.maximum(grad_norm, clip_limit)
    correction = 1.0 - jnp.power(0.5, step_count[0].astype(jnp.float32))
    kernel_rate = (KERNEL * KERNEL * IN_DIM) ** (-0.5)
    kern_out = adamw(kernels, kernel_moment, kernel_second, shard * factor, kernel_rate, correction)
    norm_out = adamw(
        norm_params, norm_moment, norm_second, grad_norms * factor, small_rate, correction
    )
    end_out = adamw(end_params, end_moment, end_second, grad_ends * factor, small_rate, correction)
    head_out = adamw(
        head_bias, head_moment, head_second, grad_head * factor, small_rate, correction
    )
    loss_value = loss_sum / count
    return (
        loss_value,
        grad_norm,
        kern_out[0],
        kern_out[1],
        kern_out[2],
        norm_out[0],
        norm_out[1],
        norm_out[2],
        end_out[0],
        end_out[1],
        end_out[2],
        head_out[0],
        head_out[1],
        head_out[2],
        jnp.stack(hidden_list),
        jnp.stack(cells_list),
    )


def solution(mesh):
    placed = (
        P("dp", None, "tile", None),
        P("dp", None, "tile", None),
        P("dp", None, "tile", None),
        P("dp"),
        P(),
        P(None, "dp", None),
        P(None, "dp", None),
        P(None, "dp", None),
        P(),
        P(),
        P(),
        P(),
        P(),
        P(),
        P(),
        P(),
        P(),
        P(None, "dp", "tile", None, None),
        P(None, "dp", "tile", None, None),
    )
    return jax.shard_map(
        per_device,
        mesh=mesh,
        in_specs=placed,
        out_specs=(
            P(),
            P(),
            P(None, "dp", None),
            P(None, "dp", None),
            P(None, "dp", None),
            P(),
            P(),
            P(),
            P(),
            P(),
            P(),
            P(),
            P(),
            P(),
            P(None, "dp", "tile", None, None),
            P(None, "dp", "tile", None, None),
        ),
        check_vma=False,
    )
```

profile of v0, /device:TPU:0, one launch (start us, length us, event | category | flops | bytes accessed | tf_op | source)
XLA Modules:
  0.0 1688.5 jit_solution(5633768059832277343)
XLA Ops:
  7.2 5.1 convert_element_type.95
  13.2 1.3 collective-permute-start.1
  14.5 3.0 collective-permute-start
  18.9 85.6 %psum.50 = f32[]{:T(128)} all-reduce(f32[]{:T(128)} %get-tuple-element.65), channel_id=1, replica_groups=mesh['tile'=4,'dp'=8] {'tile','dp'}, use_global_device_ids=true, to_apply=%region_10.11 | all-reduce | flops 1 | bytes 8 | tf_op jit(solution)/shard_map/psum | solution.py:159
  108.5 408.1 %all-gather.3.cloned.1.call-done = bf16[1,12800,1024]{2,1,0:T(8,128)(2,1)} async-done(((bf16[1,1600,1024]{2,1,0:T(8,128)(2,1)}), bf16[1,12800,1024]{2,1,0:T(8,128)(2,1)}) %all-gather.3.cloned.1.call-update) | async-done | bytes 26214416 | tf_op jit(solution)/shard_map/all_gather | solution.py:166
  516.7 10.8 fusion.3
  530.1 1.3 collective-permute-start.3
  531.4 3.0 collective-permute-start.2
  534.4 18.4 %reverse_bitcast_fusion = bf16[5,5,1024,512]{2,3,1,0:T(8,128)(2,1)} fusion(bf16[5,5,512,1024]{3,2,1,0:T(8,128)(2,1)} %bitcast.214), kind=kLoop, calls=%fused_computation.6 | loop fusion | bytes 52428800 | tf_op jit(solution)/shard_map/transpose | solution.py:93
  552.8 33.9 %copy.35 = bf16[5,5,1024,512]{3,2,1,0:T(8,128)(2,1)} copy(bf16[5,5,1024,512]{2,3,1,0:T(8,128)(2,1)} %reverse_bitcast_fusion) | data formatting | bytes 52428800 | tf_op jit(solution)/shard_map/transpose | solution.py:93
  588.8 10.8 fusion.1
  606.1 1.3 collective-permute-start.5
  607.4 3.8 collective-permute-start.4
  611.2 21.6 %fusion.11 = f32[12800,1024,1]{1,0,2:T(8,128)} fusion(bf16[1,2,32,12800]{3,2,1,0:T(8,128)(2,1)} %copy-done, bf16[1,2,32,1024]{3,2,1,0:T(8,128)(2,1)S(1)} %fusion.25), kind=kOutput, calls=%fused_computation.17 | convolution fusion | flops 1677721600 | bytes 54198272 | tf_op jit(solution)/shard_map/dot_general | solution.py:109
  633.8 10.8 fusion.13
  647.9 33.5 %fusion = f32[1,12800,1024]{2,1,0:T(8,128)} fusion(f32[12800,1024,1]{1,0,2:T(8,128)} %fusion.11, bf16[1,2,32,12800]{3,2,1,0:T(8,128)(2,1)S(1)} %copy-done.2, bf16[1,2,32,1024]{3,2,1,0:T(8,128)(2,1)S(1)} %fusion.27), kind=kOutput, calls=%fused_computation.1 | convolution fusion | flops 1690828800 | bytes 106627072 | tf_op jit(solution)/shard_map/dot_general | solution.py:109
  684.8 4.5 collective-permute-start.6
  705.7 793.9 %reduce-scatter.2.cloned.1.call-done = f32[1,1600,1024]{2,1,0:T(8,128)} async-done(((f32[1,12800,1024]{2,1,0:T(8,128)}), f32[1,1600,1024]{2,1,0:T(8,128)}) %reduce-scatter.2.cloned.1.call-update) | async-done | bytes 6553616 | tf_op jit(solution)/shard_map/reduce_scatter | solution.py:221
  1503.7 12.9 fusion.16
  1516.8 41.4 %all-reduce.12 = (f32[]{:T(128)}, f32[2,1,1024]{2,1,0:T(1,128)S(1)}, f32[3,256]{1,0:T(4,128)S(1)}, f32[1]{0:T(128)}) all-reduce(f32[]{:T(128)S(6)} %add.410, f32[2,1,1024]{2,1,0:T(1,128)S(1)} %pad_maximum_fusion.14, f32[3,256]{1,0:T(4,128)S(1)} %pad_maximum_fusion.15, f32[1]{0:T(128)} %bitcast.95), channel_id=1, replica_groups=mesh['tile'=4,'dp'=8] {'tile','dp'}, use_global_device_ids=true, to_apply=%region_8.9 | all-reduce | flops 2818 | bytes 22544 | tf_op jit(solution)/shard_map/psum | solution.py:224
  1560.1 66.4 %all-reduce.15.cloned.1.call-done = f32[1,1600,1024]{2,1,0:T(8,128)} async-done(((f32[1,1600,1024]{2,1,0:T(8,128)}), f32[1,1600,1024]{2,1,0:T(8,128)}) %all-reduce.15.cloned.1.call-update) | async-done | bytes 6553616 | tf_op jit(solution)/shard_map/psum | solution.py:222
  1626.4 5.1 multiply_reduce_fusion
  1632.9 22.0 %psum.52 = f32[]{:T(128)} all-reduce(f32[]{:T(128)} %multiply_reduce_fusion), channel_id=1, replica_groups=mesh['tile'=4,'dp'=8] {'dp'}, use_global_device_ids=true, to_apply=%region_18.19 | all-reduce | flops 1 | bytes 8 | tf_op jit(solution)/shard_map/psum | solution.py:227
  1659.0 17.3 %multiply_subtract_fusion = (f32[1,1600,1024]{2,1,0:T(8,128)}, f32[1,1600,1024]{2,1,0:T(8,128)}, f32[1,1600,1024]{2,1,0:T(8,128)}) fusion(f32[1,1600,1024]{2,1,0:T(8,128)} %param.24, f32[]{:T(128)} %bitcast.97, f32[1,1600,1024]{2,1,0:T(8,128)} %all-reduce.15.cloned.1.call-done, f32[]{:T(128)} %div.177, f32[1,1600,1024]{2,1,0:T(8,128)} %param.26, ...), kind=kLoop, calls=%fused_computation.10 | loop fusion | flops 24576000 | bytes 45875208 | tf_op jit(solution)/shard_map/sub | solution.py:130
  (289 shorter events, 40.2 us)
Async XLA Ops:
  7.2 509.5 %all-gather.3.cloned.1.call-start = ((), (), s32[]{:S(2)}) async-start(), calls=%async_computation.3 | async-start | bytes 29491200 | tf_op jit(solution)/shard_map/all_gather | solution.py:166
  12.3 5.9 copy-start.7
  12.3 5.9 copy-start.19
  12.4 1487.3 %reduce-scatter.2.cloned.1.call-start = ((), (), s32[]{:S(2)}) async-start(), calls=%async_computation.1 | async-start | bytes 58982400 | tf_op jit(solution)/shard_map/reduce_scatter | solution.py:221
  13.0 93.6 %copy-start.9 = (f32[2,32]{1,0:T(2,128)}, f32[2,32]{1,0:T(2,128)S(1)}, u32[]{:S(2)}) copy-start(f32[2,32]{1,0:T(2,128)S(1)} %get-tuple-element.135) | copy-start | bytes 772
  13.2 92.8 %collective-permute-start.1 = (bf16[1,2,32,512]{3,2,1,0:T(8,128)(2,1)S(1)}, bf16[1,2,32,512]{3,2,1,0:T(8,128)(2,1)S(1)}, u32[]{:S(2)}, u32[]{:S(2)}) collective-permute-start(bf16[1,2,32,512]{3,2,1,0:T(8,128)(2,1)S(1)} %pad_maximum_fusion.12), channel_id=1, source_target_pairs={{8,0},{16,8},{24,16},{9,1},{17,9},{25,17},{10,2},{18,10},{26,18},{... | collective-permute-start | bytes 196616 | tf_op jit(solution)/shard_map/ppermute | solution.py:23
  14.5 91.5 %collective-permute-start = (bf16[1,2,32,512]{3,2,1,0:T(8,128)(2,1)S(1)}, bf16[1,2,32,512]{3,2,1,0:T(8,128)(2,1)S(1)}, u32[]{:S(2)}, u32[]{:S(2)}) collective-permute-start(bf16[1,2,32,512]{3,2,1,0:T(8,128)(2,1)S(1)} %pad_maximum_fusion.12), channel_id=1, source_target_pairs={{0,8},{8,16},{16,24},{1,9},{9,17},{17,25},{2,10},{10,18},{18,26},{... | collective-permute-start | bytes 196616 | tf_op jit(solution)/shard_map/ppermute | solution.py:21
  530.1 56.6 %collective-permute-start.3 = (bf16[1,2,32,512]{3,2,1,0:T(8,128)(2,1)S(1)}, bf16[1,2,32,512]{3,2,1,0:T(8,128)(2,1)S(1)}, u32[]{:S(2)}, u32[]{:S(2)}) collective-permute-start(bf16[1,2,32,512]{3,2,1,0:T(8,128)(2,1)S(1)} %pad_maximum_fusion.13), channel_id=1, source_target_pairs={{8,0},{16,8},{24,16},{9,1},{17,9},{25,17},{10,2},{18,10},{26,18},{... | collective-permute-start | bytes 196616 | tf_op jit(solution)/shard_map/ppermute | solution.py:23
  531.4 55.3 %collective-permute-start.2 = (bf16[1,2,32,512]{3,2,1,0:T(8,128)(2,1)S(1)}, bf16[1,2,32,512]{3,2,1,0:T(8,128)(2,1)S(1)}, u32[]{:S(2)}, u32[]{:S(2)}) collective-permute-start(bf16[1,2,32,512]{3,2,1,0:T(8,128)(2,1)S(1)} %pad_maximum_fusion.13), channel_id=1, source_target_pairs={{0,8},{8,16},{16,24},{1,9},{9,17},{17,25},{2,10},{10,18},{18,26},{... | collective-permute-start | bytes 196616 | tf_op jit(solution)/shard_map/ppermute | solution.py:21
  601.1 1.8 copy-start.15
  602.8 41.9 %copy-start.3 = (f32[1,2,32,256]{3,2,1,0:T(8,128)}, f32[1,2,32,256]{3,2,1,0:T(8,128)S(1)}, u32[]{:S(2)}) copy-start(f32[1,2,32,256]{3,2,1,0:T(8,128)S(1)} %get-tuple-element.37) | copy-start | bytes 196612
  606.1 26.7 %collective-permute-start.5 = (bf16[1,2,32,1024]{3,2,1,0:T(8,128)(2,1)S(1)}, bf16[1,2,32,1024]{3,2,1,0:T(8,128)(2,1)S(1)}, u32[]{:S(2)}, u32[]{:S(2)}) collective-permute-start(bf16[1,2,32,1024]{3,2,1,0:T(8,128)(2,1)S(1)} %fusion.25), channel_id=1, source_target_pairs={{8,0},{16,8},{24,16},{9,1},{17,9},{25,17},{10,2},{18,10},{26,18},{... | collective-permute-start | bytes 393224 | tf_op jit(solution)/shard_map/ppermute | solution.py:23
  607.4 25.4 %collective-permute-start.4 = (bf16[1,2,32,1024]{3,2,1,0:T(8,128)(2,1)S(1)}, bf16[1,2,32,1024]{3,2,1,0:T(8,128)(2,1)S(1)}, u32[]{:S(2)}, u32[]{:S(2)}) collective-permute-start(bf16[1,2,32,1024]{3,2,1,0:T(8,128)(2,1)S(1)} %fusion.25), channel_id=1, source_target_pairs={{0,8},{8,16},{16,24},{1,9},{9,17},{17,25},{2,10},{10,18},{18,26},{... | collective-permute-start | bytes 393224 | tf_op jit(solution)/shard_map/ppermute | solution.py:21
  633.8 11.0 copy-start.6
  681.5 944.9 %all-reduce.15.cloned.1.call-start = ((), (), s32[]{:S(2)}) async-start(), calls=%async_computation.2 | async-start | bytes 13107200 | tf_op jit(solution)/shard_map/psum | solution.py:222
  683.5 9.1 collective-permute-start.7
  684.8 7.8 collective-permute-start.6
  1503.7 12.9 copy-start.10
  1560.0 97.7 %copy-start.8 = (f32[2,1,1024]{2,1,0:T(1,128)S(1)}, f32[2,1,1024]{2,1,0:T(1,128)}, u32[]{:S(2)}) copy-start(f32[2,1,1024]{2,1,0:T(1,128)} %param.27) | copy-start | bytes 24580
  1560.0 97.7 %copy-start.13 = (f32[2,1,1024]{2,1,0:T(1,128)S(1)}, f32[2,1,1024]{2,1,0:T(1,128)}, u32[]{:S(2)}) copy-start(f32[2,1,1024]{2,1,0:T(1,128)} %param.29) | copy-start | bytes 24580
  1560.0 97.7 %copy-start.14 = (f32[2,1,1024]{2,1,0:T(1,128)S(1)}, f32[2,1,1024]{2,1,0:T(1,128)}, u32[]{:S(2)}) copy-start(f32[2,1,1024]{2,1,0:T(1,128)} %param.28) | copy-start | bytes 24580
  1560.0 98.3 %copy-start.12 = (f32[3,256]{1,0:T(4,128)S(1)}, f32[3,256]{1,0:T(4,128)}, u32[]{:S(2)}) copy-start(f32[3,256]{1,0:T(4,128)} %param.30) | copy-start | bytes 9220
  1560.0 98.3 %copy-start.16 = (f32[3,256]{1,0:T(4,128)S(1)}, f32[3,256]{1,0:T(4,128)}, u32[]{:S(2)}) copy-start(f32[3,256]{1,0:T(4,128)} %param.32) | copy-start | bytes 9220
  1560.0 98.3 %copy-start.17 = (f32[3,256]{1,0:T(4,128)S(1)}, f32[3,256]{1,0:T(4,128)}, u32[]{:S(2)}) copy-start(f32[3,256]{1,0:T(4,128)} %param.31) | copy-start | bytes 9220
  (7 other events, 7.4 us)
Sparse Core Ops, SparseCore 0:
  12.5 504.1 all-gather.2
  681.6 817.9 reduce-scatter.1
  1502.0 124.3 all-reduce.14
where the time goes:
time: 1690 us
  waiting for transfers between devices  1270 us (75%)
  blocking collectives  149 us (9%)
  matrix products  100 us (6%)
  local copies, waits for them, and re-layouts  76.5 us (5%)
  other arithmetic  41.9 us (2%)
  between operations  32.4 us (2%)
  starting transfers between devices  19.7 us (1%)
    reduce_scatter x1, waiting for transfers between devices, per_device(): lax.psum_scatter(grad_kernels, 'dp', scatter_dimension=1, tiled=True)  794 us
    all_gather x1, waiting for transfers between devices, per_device(): lax.all_gather(kernels[layer_no].astype(jnp.bfloat16), 'dp', axis=0, tile...  408 us
    psum x1, blocking collectives, per_device(): count = jnp.maximum(lax.psum(jnp.sum(valid), ('tile', 'dp')), 1.0)  85.6 us
    psum x1, waiting for transfers between devices, per_device(): shard = lax.psum(shard, 'tile')  66.4 us
    dot_general x2, matrix products, layer_backward(): lax.dot_general(unfold(padded, rows, columns), gates_low.reshape(-1, gate...  55.1 us
    transpose x2, local copies, waits for them, and re-layouts, layer_backward(): flipped.transpose(0, 1, 3, 2).reshape(KERNEL * KERNEL * gate_dim, in_dim)  52.3 us
    psum x1, blocking collectives, per_device(): lax.psum((grad_norms, grad_ends, grad_head, loss_sum), ('tile', 'dp'))  41.4 us
  transfers between devices with their start and end apart: 11, of which 3 were waited for; matrix products, arithmetic and copies ran while one was open for 6% of the time, Pallas kernels for 0%

commit v1 on v0

--- a/solution.py
+++ b/solution.py
@@ -151,6 +151,32 @@
     hidden_init,
     cells_init,
 ):
+
+    def choose_the_panels(vals, ndim_at):
+        current_value = jax.lax.axis_size("dp")
+        y_new = jax.lax.axis_index("dp")
+        y, ready, formed = (current_value, y_new, vals.shape[ndim_at])
+        plain = jnp.zeros(
+            [pp * y if dev_j == ndim_at else pp for dev_j, pp in enumerate(vals.shape)], vals.dtype
+        )
+        f_next = lax.dynamic_update_slice_in_dim(plain, vals, ready * formed, axis=ndim_at)
+        d_next = a_now = vals
+        for c in tuple(range(1, y // 2 + 1)):
+            d_next = jax.lax.ppermute(
+                d_next, axis_name="dp", perm=[(dev_j, (dev_j + 1) % y) for dev_j in range(y)]
+            )
+            f_next = lax.dynamic_update_slice_in_dim(
+                f_next, d_next, (ready - c) % y * formed, axis=ndim_at
+            )
+            if 2 * c < y:
+                a_now = jax.lax.ppermute(
+                    a_now, axis_name="dp", perm=[(dev_j, (dev_j - 1) % y) for dev_j in range(y)]
+                )
+                f_next = lax.dynamic_update_slice_in_dim(
+                    f_next, a_now, (ready + c) % y * formed, axis=ndim_at
+                )
+        return f_next
+
     frame_total = observed.shape[1]
     layers = kernels.shape[0]
     frame_ids = lax.broadcasted_iota(jnp.int32, (1, frame_total), 1)
@@ -163,7 +189,7 @@
     ]
     outputs = []
     layer_no = 0
-    weight_full = lax.all_gather(kernels[layer_no].astype(jnp.bfloat16), "dp", axis=0, tiled=True)
+    weight_full = choose_the_panels(kernels[layer_no].astype(jnp.bfloat16), 0)
     outputs, outputs_low, kept, hidden, cells = layer_forward(
         weight_full,
         norm_params[0, layer_no],

time: 1690 us -> 2260 us (1.34)
  waiting for transfers between devices: 1270 us -> 1810 us
  local copies, waits for them, and re-layouts: 76.5 us -> 122 us
  blocking collectives: 149 us -> 104 us
    ppermute x0 -> x7, waiting for transfers between devices: none -> 949 us  [the longest x4 563 us: choose_the_panels(): jax.lax.ppermute(d_next, axis_name='dp', perm=[(dev_j, (dev_j + 1) % y) f...]
    all_gather x1, waiting for transfers between devices: 408 us -> 0.01 us  [per_device(): lax.all_gather(kernels[layer_no].astype(jnp.bfloat16), 'dp', axis=0, tile...]
    psum x1, blocking collectives: 85.6 us -> 40.8 us  [per_device(): count = jnp.maximum(lax.psum(jnp.sum(valid), ('tile', 'dp')), 1.0)]
  transfers between devices with their start and end apart: 11 -> 18, of which waited for: 3 -> 7; matrix products, arithmetic and copies ran while one was open for 6% -> 6% of each run, Pallas kernels for 0% -> 0%
where the time goes in v1:
time: 2260 us
  waiting for transfers between devices  1810 us (80%)
  local copies, waits for them, and re-layouts  122 us (5%)
  blocking collectives  104 us (5%)
  matrix products  101 us (4%)
  other arithmetic  45 us (2%)
  starting transfers between devices  41.6 us (2%)
  between operations  32.3 us (1%)
    reduce_scatter x1, waiting for transfers between devices, per_device(): lax.psum_scatter(grad_kernels, 'dp', scatter_dimension=1, tiled=True)  793 us
    ppermute x4, waiting for transfers between devices, choose_the_panels(): jax.lax.ppermute(d_next, axis_name='dp', perm=[(dev_j, (dev_j + 1) % y) f...  563 us
    ppermute x3, waiting for transfers between devices, choose_the_panels(): jax.lax.ppermute(a_now, axis_name='dp', perm=[(dev_j, (dev_j - 1) % y) fo...  386 us
    psum x1, waiting for transfers between devices, per_device(): shard = lax.psum(shard, 'tile')  66.4 us
    dot_general x2, matrix products, layer_backward(): lax.dot_general(unfold(padded, rows, columns), gates_low.reshape(-1, gate...  55.1 us
    transpose x2, local copies, waits for them, and re-layouts, layer_backward(): flipped.transpose(0, 1, 3, 2).reshape(KERNEL * KERNEL * gate_dim, in_dim)  52.1 us
  transfers between devices with their start and end apart: 18, of which 7 were waited for; matrix products, arithmetic and copies ran while one was open for 6% of the time, Pallas kernels for 0%

profile of v1, /device:TPU:0, one launch (start us, length us, event | category | flops | bytes accessed | tf_op | source)
XLA Modules:
  0.0 2255.1 jit_solution(9720250116042049880)
XLA Ops:
  7.2 10.3 broadcast_in_dim.22
  39.0 291.7 %collective-permute-done.2 = bf16[1600,1024]{1,0:T(8,128)(2,1)} collective-permute-done((bf16[1600,1024]{1,0:T(8,128)(2,1)S(1)}, bf16[1600,1024]{1,0:T(8,128)(2,1)}, u32[]{:S(2)}, u32[]{:S(2)}) %collective-permute-start.2) | collective-permute-done | bytes 3276832 | tf_op jit(solution)/shard_map/ppermute | solution.py:165
  333.7 117.9 %collective-permute-done.3 = bf16[1600,1024]{1,0:T(8,128)(2,1)} collective-permute-done((bf16[1600,1024]{1,0:T(8,128)(2,1)S(1)}, bf16[1600,1024]{1,0:T(8,128)(2,1)}, u32[]{:S(2)}, u32[]{:S(2)}) %collective-permute-start.3) | collective-permute-done | bytes 3276832 | tf_op jit(solution)/shard_map/ppermute | solution.py:172
  454.2 268.6 %collective-permute-done.5 = bf16[1600,1024]{1,0:T(8,128)(2,1)S(1)} collective-permute-done((bf16[1600,1024]{1,0:T(8,128)(2,1)}, bf16[1600,1024]{1,0:T(8,128)(2,1)S(1)}, u32[]{:S(2)}, u32[]{:S(2)}) %collective-permute-start.5) | collective-permute-done | bytes 3276832 | tf_op jit(solution)/shard_map/ppermute | solution.py:172
  722.9 140.6 %collective-permute-done.6 = bf16[1600,1024]{1,0:T(8,128)(2,1)S(1)} collective-permute-done((bf16[1600,1024]{1,0:T(8,128)(2,1)S(1)}, bf16[1600,1024]{1,0:T(8,128)(2,1)S(1)}, u32[]{:S(2)}, u32[]{:S(2)}) %collective-permute-start.6) | collective-permute-done | bytes 3276832 | tf_op jit(solution)/shard_map/ppermute | solution.py:165
  863.6 11.3 collective-permute-start.8
  875.0 4.0 constant_dynamic-update-slice_fusion.160
  891.2 130.3 %collective-permute-done.8 = bf16[1600,1024]{1,0:T(8,128)(2,1)S(1)} collective-permute-done((bf16[1600,1024]{1,0:T(8,128)(2,1)S(1)}, bf16[1600,1024]{1,0:T(8,128)(2,1)S(1)}, u32[]{:S(2)}, u32[]{:S(2)}) %collective-permute-start.8) | collective-permute-done | bytes 3276832 | tf_op jit(solution)/shard_map/ppermute | solution.py:165
  1023.5 10.8 fusion.79
  1041.9 40.8 %psum.50 = f32[]{:T(128)} all-reduce(f32[]{:T(128)} %get-tuple-element.67), channel_id=1, replica_groups=mesh['tile'=4,'dp'=8] {'tile','dp'}, use_global_device_ids=true, to_apply=%region_10.11 | all-reduce | flops 1 | bytes 8 | tf_op jit(solution)/shard_map/psum | solution.py:185
  1086.3 10.8 fusion.80
  1108.7 21.6 fusion.7
  1147.4 18.2 reverse_bitcast_fusion
  1165.6 33.9 %copy.35 = bf16[5,5,1024,512]{3,2,1,0:T(8,128)(2,1)} copy(bf16[5,5,1024,512]{2,3,1,0:T(8,128)(2,1)} %reverse_bitcast_fusion) | data formatting | bytes 52428800 | tf_op jit(solution)/shard_map/transpose | solution.py:93
  1199.5 11.7 fusion.9
  1215.1 33.5 %fusion = f32[1,12800,1024]{2,1,0:T(8,128)} fusion(f32[12800,1024,1]{1,0,2:T(8,128)} %fusion.7, bf16[1,2,32,12800]{3,2,1,0:T(8,128)(2,1)S(1)} %copy-done.4, bf16[1,2,32,1024]{3,2,1,0:T(8,128)(2,1)S(1)} %fusion.23), kind=kOutput, calls=%fused_computation.1 | convolution fusion | flops 1690828800 | bytes 106627072 | tf_op jit(solution)/shard_map/dot_general | solution.py:109
  1252.0 4.9 collective-permute-start.13
  1273.2 793.1 %reduce-scatter.2.cloned.1.call-done = f32[1,1600,1024]{2,1,0:T(8,128)} async-done(((f32[1,12800,1024]{2,1,0:T(8,128)}), f32[1,1600,1024]{2,1,0:T(8,128)}) %reduce-scatter.2.cloned.1.call-update) | async-done | bytes 6553616 | tf_op jit(solution)/shard_map/reduce_scatter | solution.py:247
  2070.4 12.9 fusion.12
  2083.4 41.3 %all-reduce.12 = (f32[]{:T(128)}, f32[2,1,1024]{2,1,0:T(1,128)S(1)}, f32[3,256]{1,0:T(4,128)S(1)}, f32[1]{0:T(128)}) all-reduce(f32[]{:T(128)S(6)} %add.487, f32[2,1,1024]{2,1,0:T(1,128)S(1)} %pad_maximum_fusion.14, f32[3,256]{1,0:T(4,128)S(1)} %pad_maximum_fusion.15, f32[1]{0:T(128)} %bitcast.95), channel_id=1, replica_groups=mesh['tile'=4,'dp'=8] {'tile','dp'}, use_global_device_ids=true, to_apply=%region_8.9 | all-reduce | flops 2818 | bytes 22544 | tf_op jit(solution)/shard_map/psum | solution.py:250
  2126.7 66.4 %all-reduce.15.cloned.1.call-done = f32[1,1600,1024]{2,1,0:T(8,128)} async-done(((f32[1,1600,1024]{2,1,0:T(8,128)}), f32[1,1600,1024]{2,1,0:T(8,128)}) %all-reduce.15.cloned.1.call-update) | async-done | bytes 6553616 | tf_op jit(solution)/shard_map/psum | solution.py:248
  2193.1 5.1 multiply_reduce_fusion
  2199.6 22.0 psum.52
  2225.7 17.3 multiply_subtract_fusion
  (335 shorter events, 103.9 us)
Async XLA Ops:
  7.2 1140.3 %all-gather.3.cloned.1.call-start = ((), (), s32[]{:S(2)}) async-start(), calls=%async_computation.3 | async-start | bytes 29491200 | tf_op jit(solution)/shard_map/all_gather | solution.py:223
  21.3 2045.0 %reduce-scatter.2.cloned.1.call-start = ((), (), s32[]{:S(2)}) async-start(), calls=%async_computation.1 | async-start | bytes 58982400 | tf_op jit(solution)/shard_map/reduce_scatter | solution.py:247
  23.2 307.5 %collective-permute-start.2 = (bf16[1600,1024]{1,0:T(8,128)(2,1)S(1)}, bf16[1600,1024]{1,0:T(8,128)(2,1)}, u32[]{:S(2)}, u32[]{:S(2)}) collective-permute-start(bf16[1600,1024]{1,0:T(8,128)(2,1)S(1)} %bitcast.216), channel_id=1, source_target_pairs={{0,1},{1,2},{2,3},{3,4},{4,5},{5,6},{6,7},{7,0},{8,9},{9,10},{10,1... | collective-permute-start | bytes 9830408 | tf_op jit(solution)/shard_map/ppermute | solution.py:165
  28.1 10.8 collective-permute-start.1
  29.3 9.5 collective-permute-start
  32.4 419.2 %collective-permute-start.3 = (bf16[1600,1024]{1,0:T(8,128)(2,1)S(1)}, bf16[1600,1024]{1,0:T(8,128)(2,1)}, u32[]{:S(2)}, u32[]{:S(2)}) collective-permute-start(bf16[1600,1024]{1,0:T(8,128)(2,1)S(1)} %bitcast.217), channel_id=1, source_target_pairs={{0,7},{1,0},{2,1},{3,2},{4,3},{5,4},{6,5},{7,6},{8,15},{9,8},{10,9... | collective-permute-start | bytes 9830408 | tf_op jit(solution)/shard_map/ppermute | solution.py:172
  37.6 295.9 %copy-start.13 = (f32[2,32]{1,0:T(2,128)S(1)}, f32[2,32]{1,0:T(2,128)}, u32[]{:S(2)}) copy-start(f32[2,32]{1,0:T(2,128)} %copy-done.12) | copy-start | bytes 772
  37.6 296.0 %copy-start.7 = (f32[1,1,2,32,256]{4,3,2,1,0:T(8,128)S(1)}, f32[1,1,2,32,256]{4,3,2,1,0:T(8,128)}, u32[]{:S(2)}) copy-start(f32[1,1,2,32,256]{4,3,2,1,0:T(8,128)} %param.36) | copy-start | bytes 196612
  330.7 121.5 %collective-permute-start.4 = (bf16[1600,1024]{1,0:T(8,128)(2,1)}, bf16[1600,1024]{1,0:T(8,128)(2,1)S(1)}, u32[]{:S(2)}, u32[]{:S(2)}) collective-permute-start(bf16[1600,1024]{1,0:T(8,128)(2,1)} %collective-permute-done.2), channel_id=1, source_target_pairs={{0,1},{1,2},{2,3},{3,4},{4,5},{5,6},{6,7},{7,0},{8,9},{9,10},{10,1... | collective-permute-start | bytes 9830408 | tf_op jit(solution)/shard_map/ppermute | solution.py:165
  451.6 271.2 %collective-permute-start.5 = (bf16[1600,1024]{1,0:T(8,128)(2,1)}, bf16[1600,1024]{1,0:T(8,128)(2,1)S(1)}, u32[]{:S(2)}, u32[]{:S(2)}) collective-permute-start(bf16[1600,1024]{1,0:T(8,128)(2,1)} %collective-permute-done.3), channel_id=1, source_target_pairs={{0,7},{1,0},{2,1},{3,2},{4,3},{5,4},{6,5},{7,6},{8,15},{9,8},{10,9... | collective-permute-start | bytes 9830408 | tf_op jit(solution)/shard_map/ppermute | solution.py:172
  452.2 411.4 %collective-permute-start.6 = (bf16[1600,1024]{1,0:T(8,128)(2,1)S(1)}, bf16[1600,1024]{1,0:T(8,128)(2,1)S(1)}, u32[]{:S(2)}, u32[]{:S(2)}) collective-permute-start(bf16[1600,1024]{1,0:T(8,128)(2,1)S(1)} %collective-permute-done.4), channel_id=1, source_target_pairs={{0,1},{1,2},{2,3},{3,4},{4,5},{5,6},{6,7},{7,0},{8,9},{9,10},{10,1... | collective-permute-start | bytes 9830408 | tf_op jit(solution)/shard_map/ppermute | solution.py:165
  453.9 268.9 %copy-start.30 = (f32[64]{0:T(128)S(1)}, f32[64]{0:T(128)}, u32[]{:S(2)}) copy-start(f32[64]{0:T(128)} %mul.817) | copy-start | bytes 772
  454.1 409.5 %copy-start.3 = (bf16[1,2,32,12800]{3,2,1,0:T(8,128)(2,1)}, bf16[1,2,32,12800]{3,2,1,0:T(8,128)(2,1)S(1)}, u32[]{:S(2)}) copy-start(bf16[1,2,32,12800]{3,2,1,0:T(8,128)(2,1)S(1)} %get-tuple-element.80) | copy-start | bytes 4915204
  722.8 166.4 %collective-permute-start.7 = (bf16[1600,1024]{1,0:T(8,128)(2,1)S(1)}, bf16[1600,1024]{1,0:T(8,128)(2,1)S(1)}, u32[]{:S(2)}, u32[]{:S(2)}) collective-permute-start(bf16[1600,1024]{1,0:T(8,128)(2,1)S(1)} %collective-permute-done.5), channel_id=1, source_target_pairs={{0,7},{1,0},{2,1},{3,2},{4,3},{5,4},{6,5},{7,6},{8,15},{9,8},{10,9... | collective-permute-start | bytes 9830408 | tf_op jit(solution)/shard_map/ppermute | solution.py:172
  863.6 157.9 %collective-permute-start.8 = (bf16[1600,1024]{1,0:T(8,128)(2,1)S(1)}, bf16[1600,1024]{1,0:T(8,128)(2,1)S(1)}, u32[]{:S(2)}, u32[]{:S(2)}) collective-permute-start(bf16[1600,1024]{1,0:T(8,128)(2,1)S(1)} %collective-permute-done.6), channel_id=1, source_target_pairs={{0,1},{1,2},{2,3},{3,4},{4,5},{5,6},{6,7},{7,0},{8,9},{9,10},{10,1... | collective-permute-start | bytes 9830408 | tf_op jit(solution)/shard_map/ppermute | solution.py:165
  1036.9 47.2 %collective-permute-start.10 = (bf16[1,2,32,512]{3,2,1,0:T(8,128)(2,1)S(1)}, bf16[1,2,32,512]{3,2,1,0:T(8,128)(2,1)S(1)}, u32[]{:S(2)}, u32[]{:S(2)}) collective-permute-start(bf16[1,2,32,512]{3,2,1,0:T(8,128)(2,1)S(1)} %pad_maximum_fusion.13), channel_id=1, source_target_pairs={{8,0},{16,8},{24,16},{9,1},{17,9},{25,17},{10,2},{18,10},{26,18},{... | collective-permute-start | bytes 196616 | tf_op jit(solution)/shard_map/ppermute | solution.py:23
  1038.2 45.9 %collective-permute-start.9 = (bf16[1,2,32,512]{3,2,1,0:T(8,128)(2,1)S(1)}, bf16[1,2,32,512]{3,2,1,0:T(8,128)(2,1)S(1)}, u32[]{:S(2)}, u32[]{:S(2)}) collective-permute-start(bf16[1,2,32,512]{3,2,1,0:T(8,128)(2,1)S(1)} %pad_maximum_fusion.13), channel_id=1, source_target_pairs={{0,8},{8,16},{16,24},{1,9},{9,17},{17,25},{2,10},{10,18},{18,26},{... | collective-permute-start | bytes 196616 | tf_op jit(solution)/shard_map/ppermute | solution.py:21
  1100.3 110.9 %copy-start.5 = (f32[1,2,32,256]{3,2,1,0:T(8,128)}, f32[1,2,32,256]{3,2,1,0:T(8,128)S(1)}, u32[]{:S(2)}) copy-start(f32[1,2,32,256]{3,2,1,0:T(8,128)S(1)} %get-tuple-element.37) | copy-start | bytes 196612
  1104.1 26.2 %collective-permute-start.12 = (bf16[1,2,32,1024]{3,2,1,0:T(8,128)(2,1)S(1)}, bf16[1,2,32,1024]{3,2,1,0:T(8,128)(2,1)S(1)}, u32[]{:S(2)}, u32[]{:S(2)}) collective-permute-start(bf16[1,2,32,1024]{3,2,1,0:T(8,128)(2,1)S(1)} %fusion.21), channel_id=1, source_target_pairs={{8,0},{16,8},{24,16},{9,1},{17,9},{25,17},{10,2},{18,10},{26,18},{... | collective-permute-start | bytes 393224 | tf_op jit(solution)/shard_map/ppermute | solution.py:23
  1105.4 24.9 %collective-permute-start.11 = (bf16[1,2,32,1024]{3,2,1,0:T(8,128)(2,1)S(1)}, bf16[1,2,32,1024]{3,2,1,0:T(8,128)(2,1)S(1)}, u32[]{:S(2)}, u32[]{:S(2)}) collective-permute-start(bf16[1,2,32,1024]{3,2,1,0:T(8,128)(2,1)S(1)} %fusion.21), channel_id=1, source_target_pairs={{0,8},{8,16},{16,24},{1,9},{9,17},{17,25},{2,10},{10,18},{18,26},{... | collective-permute-start | bytes 393224 | tf_op jit(solution)/shard_map/ppermute | solution.py:21
  1248.6 944.5 %all-reduce.15.cloned.1.call-start = ((), (), s32[]{:S(2)}) async-start(), calls=%async_computation.2 | async-start | bytes 13107200 | tf_op jit(solution)/shard_map/psum | solution.py:248
  1250.7 9.5 collective-permute-start.14
  1252.0 8.2 collective-permute-start.13
  2126.7 98.4 %copy-start.25 = (f32[3,256]{1,0:T(4,128)S(1)}, f32[3,256]{1,0:T(4,128)}, u32[]{:S(2)}) copy-start(f32[3,256]{1,0:T(4,128)} %param.32) | copy-start | bytes 9220
  (26 other events, 711.2 us)
Sparse Core Ops, SparseCore 0:
  21.4 1004.2 all-gather.2
  1248.7 817.5 reduce-scatter.1
  2068.7 124.3 all-reduce.14
